TPU v7x, 32 devices: a whole 2x2x4 slice. The times are simulated.
32 devices in a mesh: seq: 8 (over z, y), chan: 4 (over x, core).
Axes of the slice: x: 2, y: 2, z: 4, core: 2. Of those that a mesh axis runs over, the one named last changes fastest.
Arguments:
- proj_in: bfloat16 [3, 1024, 4096], P(None, 'seq', 'chan'), may hold values from -6 to 6
- taps: float32 [3, 3, 4096], P(None, None, 'chan'), may hold values from -3 to 3
- long_filter: float32 [1024, 256], P('seq'), may hold values from -6 to 6
- out_grad: bfloat16 [1024, 4096], P('seq', 'chan'), may hold values from -0.1875 to 0.1875
Outputs:
- input_grad: bfloat16 [3, 1024, 4096], P(None, 'seq', 'chan')
- long_grad: float32 [1024, 256], P('seq', 'chan')
- tap_grad: float32 [3, 3, 4096], P(None, None, 'chan')
All inputs are finite; a program needn't handle non-finite values.
Results may differ from a plain program's by a relative error of at most 0.001.
Values may be sent and summed in bfloat16 or wider, within the bound.
A program may use at most 64 MiB of HBM per device.

v0:
```python
import math
import jax
import jax.numpy as jnp
from jax import lax
from jax.sharding import PartitionSpec as P


def shifted(x, axis, by):
    devices = lax.axis_size(axis)
    pairs = [(i, i + by) for i in range(devices) if 0 <= i + by < devices]
    return lax.ppermute(x, axis, pairs)


def angle_table(left_index, right_index, period):
    product = left_index[:, None] * right_index[None, :] % period
    phase = product.astype(jnp.float32) * (2.0 * math.pi / period)
    return (jnp.cos(phase), jnp.sin(phase))


def contract(pattern, factor_table, operand):
    return jnp.einsum(pattern, factor_table, operand, precision=lax.Precision.HIGHEST)


def steps_of(count):
    return jnp.arange(count, dtype=jnp.int32)


def whole_forward(signal, seq_width):
    tok_rows, stack_count, channels = signal.shape
    period = 2 * seq_width * tok_rows
    narrow = channels // seq_width
    arrived = lax.all_to_all(signal, "seq", split_axis=2, concat_axis=0, tiled=True)
    laid = arrived.reshape(seq_width, tok_rows, stack_count, narrow).transpose(2, 3, 0, 1)
    cos_step, sin_step = angle_table(steps_of(2 * seq_width), steps_of(seq_width), 2 * seq_width)
    real_part = contract("qm,ncmj->ncqj", cos_step, laid)
    imag_part = -contract("qm,ncmj->ncqj", sin_step, laid)
    cos_turn, sin_turn = angle_table(steps_of(2 * seq_width), steps_of(tok_rows), period)
    turned_re = real_part * cos_turn + imag_part * sin_turn
    turned_im = imag_part * cos_turn - real_part * sin_turn
    cos_row, sin_row = angle_table(steps_of(tok_rows), steps_of(tok_rows), tok_rows)
    spec_re = contract("rj,ncqj->ncqr", cos_row, turned_re) + contract(
        "rj,ncqj->ncqr", sin_row, turned_im
    )
    spec_im = contract("rj,ncqj->ncqr", cos_row, turned_im) - contract(
        "rj,ncqj->ncqr", sin_row, turned_re
    )
    return (spec_re, spec_im)


def whole_inverse(spec_re, spec_im, seq_width):
    stack_count, narrow, freq_count, tok_rows = spec_re.shape
    period = 2 * seq_width * tok_rows
    cos_row, sin_row = angle_table(steps_of(tok_rows), steps_of(tok_rows), tok_rows)
    back_re = contract("rj,ncqr->ncqj", cos_row, spec_re) - contract(
        "rj,ncqr->ncqj", sin_row, spec_im
    )
    back_im = contract("rj,ncqr->ncqj", sin_row, spec_re) + contract(
        "rj,ncqr->ncqj", cos_row, spec_im
    )
    cos_turn, sin_turn = angle_table(steps_of(freq_count), steps_of(tok_rows), period)
    turned_re = back_re * cos_turn - back_im * sin_turn
    turned_im = back_re * sin_turn + back_im * cos_turn
    cos_step, sin_step = angle_table(steps_of(seq_width), steps_of(freq_count), freq_count)
    signal = contract("mq,ncqj->ncmj", cos_step, turned_re) - contract(
        "mq,ncqj->ncmj", sin_step, turned_im
    )
    signal = (
        (signal / period).transpose(2, 3, 0, 1).reshape(seq_width * tok_rows, stack_count, narrow)
    )
    return lax.all_to_all(signal, "seq", split_axis=0, concat_axis=2, tiled=True)


def member(values, index, stack_axis):
    return lax.index_in_dim(values, index, stack_axis, keepdims=False)


def shards(proj_in, taps, long_filter, out_grad):
    stream_count, tok_rows, channels = proj_in.shape
    tap_count = taps.shape[1]
    groups = long_filter.shape[1]
    seq_width = lax.axis_size("seq")
    lower_rim = shifted(proj_in[:, tok_rows - (tap_count - 1) :, :], "seq", 1)
    extended = jnp.concatenate([lower_rim, proj_in], axis=1).astype(jnp.float32)
    lagged = [
        extended[:, tap_count - 1 - lag_step : tap_count - 1 - lag_step + tok_rows, :]
        for lag_step in range(tap_count)
    ]
    featured = taps[:, 0, None, :] * lagged[0]
    for lag_step in range(1, tap_count):
        featured = featured + taps[:, lag_step, None, :] * lagged[lag_step]
    query_rows, key_rows, value_rows = (featured[0], featured[1], featured[2])
    mixed_rows = key_rows * value_rows
    upstream = out_grad.astype(jnp.float32)
    conv_grad = upstream * query_rows
    tiled_filter = jnp.tile(long_filter, (1, channels // groups))
    signals = jnp.stack([mixed_rows, conv_grad, tiled_filter], axis=1)
    data_re, data_im = whole_forward(signals, seq_width)
    stack_axis = 0
    mix_re, mix_im = (member(data_re, 0, stack_axis), member(data_im, 0, stack_axis))
    grad_re, grad_im = (member(data_re, 1, stack_axis), member(data_im, 1, stack_axis))
    filt_re, filt_im = (member(data_re, 2, stack_axis), member(data_im, 2, stack_axis))
    conv_re = filt_re * mix_re - filt_im * mix_im
    conv_im = filt_re * mix_im + filt_im * mix_re
    back_re = filt_re * grad_re + filt_im * grad_im
    back_im = filt_re * grad_im - filt_im * grad_re
    corr_re = grad_re * mix_re + grad_im * mix_im
    corr_im = grad_im * mix_re - grad_re * mix_im
    prod_re = jnp.stack([conv_re, back_re, corr_re], axis=stack_axis)
    prod_im = jnp.stack([conv_im, back_im, corr_im], axis=stack_axis)
    outputs = whole_inverse(prod_re, prod_im, seq_width)
    conv_out, mixed_grad = (outputs[:, 0], outputs[:, 1])
    filt_grad = jnp.sum(outputs[:, 2].reshape(tok_rows, channels // groups, groups), axis=1)
    long_grad = lax.psum_scatter(filt_grad, "chan", scatter_dimension=1, tiled=True)
    feature_grad = jnp.stack(
        [upstream * conv_out, mixed_grad * value_rows, mixed_grad * key_rows], axis=0
    )
    upper_rim = shifted(feature_grad[:, : tap_count - 1, :], "seq", -1)
    trailing = jnp.concatenate([feature_grad, upper_rim], axis=1)
    input_grad = taps[:, 0, None, :] * feature_grad
    for lag_step in range(1, tap_count):
        input_grad = (
            input_grad + taps[:, lag_step, None, :] * trailing[:, lag_step : lag_step + tok_rows]
        )
    partial_taps = jnp.stack(
        [jnp.sum(feature_grad * lagged[lag_step], axis=1) for lag_step in range(tap_count)], axis=1
    )
    tap_grad = lax.psum(partial_taps, "seq") / math.sqrt(seq_width * tok_rows)
    return (input_grad.astype(jnp.bfloat16), long_grad, tap_grad)


def solution(mesh):
    return jax.shard_map(
        shards,
        mesh=mesh,
        in_specs=(P(None, "seq", "chan"), P(None, None, "chan"), P("seq", None), P("seq", "chan")),
        out_specs=(P(None, "seq", "chan"), P("seq", "chan"), P(None, None, "chan")),
        check_vma=False,
    )
```

profile of v0, /device:TPU:0, one launch (start us, length us, event | category | flops | bytes accessed | tf_op | source)
XLA Modules:
  0.0 260.6 jit_solution(12826561988551582519)
XLA Ops:
  8.0 4.9 %collective-permute-start = (bf16[3,2,1024]{2,1,0:T(2,128)(2,1)S(1)}, bf16[3,2,1024]{2,1,0:T(2,128)(2,1)S(1)}, u32[]{:S(2)}, u32[]{:S(2)}) collective-permute-start(bf16[3,2,1024]{2,1,0:T(2,128)(2,1)S(1)} %slice.70), channel_id=1, source_target_pairs={{0,4},{4,8},{8,12},{12,16},{16,20},{20,24},{24,28},{1,5},{5,9},{9,... | collective-permute-start | bytes 36872 | tf_op jit(solution)/shard_map/ppermute | solution.py:11
  14.4 2.3 copy.34
  22.7 3.2 %multiply_add_fusion = f32[3,128,1024]{1,2,0:T(8,128)S(1)} fusion(f32[3,130,1024]{1,2,0:T(8,128)S(1)} %maximum_convert_fusion, f32[3,1024]{1,0:T(4,128)S(1)} %get-tuple-element.26, f32[3,1024]{1,0:T(4,128)} %get-tuple-element.27, f32[3,1024]{1,0:T(4,128)S(1)} %bitcast.116), kind=kLoop, calls=%fused_computation.57 | loop fusion | flops 1966080 | bytes 6328320 | tf_op jit(solution)/shard_map/add | solution.py:90
  27.1 2.7 %pad_maximum_fusion.3 = f32[128,3,1024]{0,1,2:T(4,128)} fusion(f32[128,1,1024]{0,1,2:T(1,128)S(1)} %bitcast.113, f32[128,1,1024]{0,1,2:T(1,128)S(1)} %bitcast.114, f32[128,1,1024]{0,1,2:T(1,128)S(1)} %bitcast.112), kind=kLoop, calls=%fused_computation.33 | loop fusion | flops 786432 | bytes 3145728 | tf_op jit(solution)/shard_map/stack | solution.py:96
  29.8 4.9 %all-to-all-start = ((f32[128,3,1024]{0,1,2:T(4,128)}), f32[128,3,1024]{0,1,2:T(4,128)}, u32[]{:S(2)}, u32[]{:S(2)}) async-start(f32[128,3,1024]{0,1,2:T(4,128)} %pad_maximum_fusion.3), calls=%async_computation | async-start | bytes 4194304 | tf_op jit(solution)/shard_map/all_to_all | solution.py:32
  34.9 47.8 %all-to-all-done = f32[128,3,1024]{0,1,2:T(4,128)} async-done(((f32[128,3,1024]{0,1,2:T(4,128)}), f32[128,3,1024]{0,1,2:T(4,128)}, u32[]{:S(2)}, u32[]{:S(2)}) %all-to-all-start) | async-done | bytes 1572896 | tf_op jit(solution)/shard_map/all_to_all | solution.py:32
  82.7 5.1 %fusion.41 = f32[3,128,128,16]{2,3,1,0:T(8,128)S(1)} fusion(f32[128,3,8,128]{0,1,3,2:T(4,128)} %bitcast.5), kind=kOutput, calls=%fused_computation.45 | convolution fusion | flops 75499264 | bytes 4718592 | tf_op jit(solution)/shard_map/qm,ncmj->ncqj/dot_general | solution.py:21
  87.8 5.7 %fusion = (f32[3,128,16,128]{3,2,1,0:T(8,128)S(1)}, f32[3,128,16,128]{3,2,1,0:T(8,128)S(1)}) fusion(f32[3,128,128,16]{2,3,1,0:T(8,128)S(1)} %fusion.41, f32[16,128]{1,0:T(8,128)S(1)} %get-tuple-element.28, f32[16,128]{1,0:T(8,128)S(1)} %get-tuple-element.29, f32[128,3,8,128]{0,1,3,2:T(4,128)} %bitcast.5), kind=kOutput, calls=%fused_computation.5 | convolution fusion | flops 81004288 | bytes 11026432 | tf_op jit(solution)/shard_map/qm,ncmj->ncqj/dot_general | solution.py:21
  93.5 3.6 %fusion.18 = f32[3,128,16,128]{3,1,2,0:T(8,128)S(1)} fusion(f32[3,128,16,128]{3,2,1,0:T(8,128)S(1)} %get-tuple-element.13), kind=kOutput, calls=%fused_computation.25 | convolution fusion | flops 1208188928 | bytes 6291456 | tf_op jit(solution)/shard_map/rj,ncqj->ncqr/dot_general | solution.py:21
  97.2 3.9 %fusion.20 = f32[3,128,16,128]{3,1,2,0:T(8,128)S(1)} fusion(f32[3,128,16,128]{3,2,1,0:T(8,128)S(1)} %get-tuple-element.13), kind=kOutput, calls=%fused_computation.27 | convolution fusion | flops 1208188928 | bytes 6291456 | tf_op jit(solution)/shard_map/rj,ncqj->ncqr/dot_general | solution.py:21
  101.1 3.7 %fusion.29 = f32[3,128,16,128]{3,1,2,0:T(8,128)S(1)} fusion(f32[3,128,16,128]{3,1,2,0:T(8,128)S(1)} %fusion.18, f32[3,128,16,128]{3,2,1,0:T(8,128)S(1)} %get-tuple-element.12), kind=kOutput, calls=%fused_computation.35 | convolution fusion | flops 1208975360 | bytes 9437184 | tf_op jit(solution)/shard_map/rj,ncqj->ncqr/dot_general | solution.py:21
  104.8 3.7 %fusion.26 = f32[3,128,16,128]{3,1,2,0:T(8,128)S(1)} fusion(f32[3,128,16,128]{3,1,2,0:T(8,128)S(1)} %fusion.20, f32[3,128,16,128]{3,2,1,0:T(8,128)S(1)} %get-tuple-element.12), kind=kOutput, calls=%fused_computation.34 | convolution fusion | flops 1208975360 | bytes 9437184 | tf_op jit(solution)/shard_map/rj,ncqj->ncqr/dot_general | solution.py:21
  110.9 4.6 %fusion.10 = f32[3,128,16,128]{3,2,1,0:T(8,128)S(1)} fusion(f32[3,128,16,128]{3,1,2,0:T(8,128)S(1)} %pad_maximum_fusion.1), kind=kOutput, calls=%fused_computation.17 | convolution fusion | flops 1208188928 | bytes 6291456 | tf_op jit(solution)/shard_map/rj,ncqr->ncqj/dot_general | solution.py:21
  115.5 4.7 %fusion.12 = f32[3,128,16,128]{3,2,1,0:T(8,128)S(1)} fusion(f32[3,128,16,128]{3,1,2,0:T(8,128)S(1)} %pad_maximum_fusion.1), kind=kOutput, calls=%fused_computation.19 | convolution fusion | flops 1208188928 | bytes 6291456 | tf_op jit(solution)/shard_map/rj,ncqr->ncqj/dot_general | solution.py:21
  120.4 4.8 %fusion.35 = f32[3,128,16,128]{3,2,1,0:T(8,128)S(1)} fusion(f32[3,128,16,128]{3,2,1,0:T(8,128)S(1)} %fusion.10, f32[3,128,16,128]{3,1,2,0:T(8,128)S(1)} %pad_maximum_fusion), kind=kOutput, calls=%fused_computation.37 | convolution fusion | flops 1208975360 | bytes 9437184 | tf_op jit(solution)/shard_map/rj,ncqr->ncqj/dot_general | solution.py:21
  125.2 4.6 %fusion.32 = f32[3,128,16,128]{3,2,1,0:T(8,128)S(1)} fusion(f32[3,128,16,128]{3,2,1,0:T(8,128)S(1)} %fusion.12, f32[3,128,16,128]{3,1,2,0:T(8,128)S(1)} %pad_maximum_fusion), kind=kOutput, calls=%fused_computation.36 | convolution fusion | flops 1208975360 | bytes 9437184 | tf_op jit(solution)/shard_map/rj,ncqr->ncqj/dot_general | solution.py:21
  132.0 3.4 %multiply_bitcast_fusion = f32[8,128,3,128]{1,0,3,2:T(8,128)} fusion(f32[3,128,128,8]{2,3,1,0:T(8,128)S(1)} %fusion.2, f32[3,128,16,128]{3,2,1,0:T(8,128)S(1)} %fusion.35, f32[3,128,16,128]{3,2,1,0:T(8,128)S(1)} %fusion.32, f32[16,128]{1,0:T(8,128)S(1)} %get-tuple-element.28, f32[16,128]{1,0:T(8,128)S(1)} %get-tuple-element.29), kind=kOutput, calls=%fused_computation.52 | convolution fusion | flops 78644992 | bytes 9453568 | tf_op jit(solution)/shard_map/mq,ncqj->ncmj/dot_general | solution.py:21
  135.4 3.6 %copy.67 = f32[8,128,3,128]{3,2,1,0:T(4,128)} copy(f32[8,128,3,128]{1,0,3,2:T(8,128)} %multiply_bitcast_fusion) | data formatting | bytes 3145728 | tf_op jit(solution)/shard_map/reshape | solution.py:68
  138.9 52.2 %all_to_all.30 = f32[1024,3,128]{2,1,0:T(4,128)} all-to-all(f32[1024,3,128]{2,1,0:T(4,128)} %bitcast.106), channel_id=1, replica_groups=mesh['seq'=8,'chan'=4] {'seq'}, dimensions={0} | all-to-all | bytes 3145728 | tf_op jit(solution)/shard_map/all_to_all | solution.py:70
  191.2 2.7 %copy.48 = f32[8,128,3,128]{1,3,0,2:T(8,128)} copy(f32[8,128,3,128]{3,2,1,0:T(4,128)} %bitcast.107) | data formatting | bytes 3145728 | tf_op jit(solution)/shard_map/all_to_all | solution.py:70
  207.4 2.2 pad_maximum_fusion.2
  209.7 5.2 %multiply_reduce_fusion.2 = (f32[3,1024]{1,0:T(4,128)S(1)}, f32[3,1024]{1,0:T(4,128)S(1)}, f32[3,1024]{1,0:T(4,128)S(1)}, bf16[3,128,1024]{1,2,0:T(8,128)(2,1)}) fusion(f32[3,130,1024]{1,2,0:T(8,128)S(1)} %maximum_convert_fusion, f32[1,128,1024]{1,2,0:T(8,128)S(1)} %copy-done.4, f32[1,128,1024]{1,2,0:T(8,128)S(1)} %copy-done.2, ...), kind=kLoop, calls=%fused_computation.51 | loop fusion | flops 5495808 | bytes 10297344 | tf_op jit(solution)/shard_map/reduce_sum | solution.py:125
  214.9 35.7 %psum.7 = f32[3,3,1024]{2,0,1:T(4,128)S(1)} all-reduce(f32[3,3,1024]{2,0,1:T(4,128)S(1)} %pad_maximum_fusion.5), channel_id=1, replica_groups=mesh['seq'=8,'chan'=4] {'seq'}, use_global_device_ids=true, to_apply=%region_5.6 | all-reduce | flops 9216 | bytes 73728 | tf_op jit(solution)/shard_map/psum | solution.py:127
  251.3 2.3 copy.51
  (53 shorter events, 28.7 us)
Async XLA Ops:
  8.0 11.5 %collective-permute-start = (bf16[3,2,1024]{2,1,0:T(2,128)(2,1)S(1)}, bf16[3,2,1024]{2,1,0:T(2,128)(2,1)S(1)}, u32[]{:S(2)}, u32[]{:S(2)}) collective-permute-start(bf16[3,2,1024]{2,1,0:T(2,128)(2,1)S(1)} %slice.70), channel_id=1, source_target_pairs={{0,4},{4,8},{8,12},{12,16},{16,20},{20,24},{24,28},{1,5},{5,9},{9,... | collective-permute-start | bytes 36872 | tf_op jit(solution)/shard_map/ppermute | solution.py:11
  20.7 2.0 copy-start.8
  25.8 1.2 copy-start
  29.8 52.9 %all-to-all-start = ((f32[128,3,1024]{0,1,2:T(4,128)}), f32[128,3,1024]{0,1,2:T(4,128)}, u32[]{:S(2)}, u32[]{:S(2)}) async-start(f32[128,3,1024]{0,1,2:T(4,128)} %pad_maximum_fusion.3), calls=%async_computation | async-start | bytes 4194304 | tf_op jit(solution)/shard_map/all_to_all | solution.py:32
  34.7 218.9 %reduce-scatter.2.cloned.1.call-start = ((), (), s32[]{:S(2)}) async-start(), calls=%async_computation.3 | async-start | bytes 163840 | tf_op jit(solution)/shard_map/reduce_scatter | solution.py:113
  195.3 1.5 copy-start.1
  195.3 2.8 %copy-start.3 = (f32[1,128,1024]{1,2,0:T(8,128)}, f32[1,128,1024]{1,2,0:T(8,128)S(1)}, u32[]{:S(2)}) copy-start(f32[1,128,1024]{1,2,0:T(8,128)S(1)} %get-tuple-element.21) | copy-start | bytes 1572868
  196.8 1.3 copy-start.5
  200.0 5.7 %collective-permute-start.1 = (f32[3,2,1024]{2,1,0:T(2,128)S(1)}, f32[3,2,1024]{2,1,0:T(2,128)S(1)}, u32[]{:S(2)}, u32[]{:S(2)}) collective-permute-start(f32[3,2,1024]{2,1,0:T(2,128)S(1)} %copy.49), channel_id=1, source_target_pairs={{4,0},{8,4},{12,8},{16,12},{20,16},{24,20},{28,24},{5,1},{9,5},{13... | collective-permute-start | bytes 73736 | tf_op jit(solution)/shard_map/ppermute | solution.py:11
  207.4 2.2 copy-start.2
  207.4 2.2 copy-start.4
  207.4 2.3 copy-start.6
  207.4 2.3 copy-start.7
  207.4 2.3 copy-start.9
Sparse Core Ops, SparseCore 0:
  205.0 19.6 reduce-scatter.1
where the time goes:
time: 265 us; the launch traced here: 261 us
  blocking collectives  87.9 us (33%)
  matrix products  49.9 us (19%)
  waiting for transfers between devices  48.6 us (18%)
  local copies, waits for them, and re-layouts  24.4 us (9%)
  other arithmetic  23.9 us (9%)
  between operations  14.6 us (6%)
  starting transfers between devices  11.3 us (4%)
    all_to_all x1, blocking collectives, whole_inverse(): lax.all_to_all(signal, 'seq', split_axis=0, concat_axis=2, tiled=True)  52.2 us
    dot_general x12, matrix products, contract(): jnp.einsum(pattern, factor_table, operand, precision=lax.Precision.HIGHEST)  49.9 us
    all_to_all x1, waiting for transfers between devices, whole_forward(): lax.all_to_all(signal, 'seq', split_axis=2, concat_axis=0, tiled=True)  47.8 us
    psum x1, blocking collectives, shards(): tap_grad = lax.psum(partial_taps, 'seq') / math.sqrt(seq_width * tok_rows)  35.7 us
    unnamed x27, local copies, waits for them, and re-layouts  9.76 us
    ppermute x2, starting transfers between devices, shifted(): return lax.ppermute(x, axis, pairs)  6.16 us
  transfers between devices with their start and end apart: 4, of which 2 were waited for; matrix products, arithmetic and copies ran while one was open for 9% of the time, Pallas kernels for 0%

commit v1 on v0

--- a/solution.py
+++ b/solution.py
@@ -67,7 +67,10 @@
     signal = (
         (signal / period).transpose(2, 3, 0, 1).reshape(seq_width * tok_rows, stack_count, narrow)
     )
-    return lax.all_to_all(signal, "seq", split_axis=0, concat_axis=2, tiled=True)
+    return jnp.concatenate(
+        lax.all_to_all(jnp.stack(jnp.split(signal, lax.axis_size("seq"), axis=0)), "seq", 0, 0),
+        axis=2,
+    )
 
 
 def member(values, index, stack_axis):

time: 265 us -> 244 us (0.921)
  blocking collectives: 87.9 us -> 76.6 us
  other arithmetic: 23.9 us -> 18.5 us
    all_to_all x1, blocking collectives: 52.2 us -> 40.7 us  [whole_inverse(): lax.all_to_all(jnp.stack(jnp.split(signal, lax.axis_size('seq'), axis=0))...]
    reshape x1 -> x0, local copies, waits for them, and re-layouts: 3.57 us -> none  [whole_inverse(): (signal / period).transpose(2, 3, 0, 1)]
    unnamed x27 -> x31, local copies, waits for them, and re-layouts: 9.76 us -> 10.6 us
where the time goes in v1:
time: 244 us; the launch traced here: 240 us
  blocking collectives  76.6 us (31%)
  matrix products  48.8 us (20%)
  waiting for transfers between devices  48.6 us (20%)
  local copies, waits for them, and re-layouts  21.9 us (9%)
  other arithmetic  18.5 us (8%)
  between operations  14.6 us (6%)
  starting transfers between devices  11.3 us (5%)
    dot_general x12, matrix products, contract(): jnp.einsum(pattern, factor_table, operand, precision=lax.Precision.HIGHEST)  48.8 us
    all_to_all x1, waiting for transfers between devices, whole_forward(): lax.all_to_all(signal, 'seq', split_axis=2, concat_axis=0, tiled=True)  47.8 us
    all_to_all x1, blocking collectives, whole_inverse(): lax.all_to_all(jnp.stack(jnp.split(signal, lax.axis_size('seq'), axis=0))...  40.7 us
    psum x1, blocking collectives, shards(): tap_grad = lax.psum(partial_taps, 'seq') / math.sqrt(seq_width * tok_rows)  35.9 us
    unnamed x31, local copies, waits for them, and re-layouts  10.6 us
    ppermute x2, starting transfers between devices, shifted(): return lax.ppermute(x, axis, pairs)  6.16 us
    reduce_sum x1, other arithmetic, shards(): jnp.sum(feature_grad * lagged[lag_step], axis=1)  5.17 us
    all_to_all x1, starting transfers between devices, whole_forward(): lax.all_to_all(signal, 'seq', split_axis=2, concat_axis=0, tiled=True)  4.88 us
  transfers between devices with their start and end apart: 4, of which 2 were waited for; matrix products, arithmetic and copies ran while one was open for 9% of the time, Pallas kernels for 0%

profile of v1, /device:TPU:0, one launch (start us, length us, event | category | flops | bytes accessed | tf_op | source)
XLA Modules:
  0.0 240.2 jit_solution(8102812210372542458)
XLA Ops:
  8.0 4.9 %collective-permute-start = (bf16[3,2,1024]{2,1,0:T(2,128)(2,1)S(1)}, bf16[3,2,1024]{2,1,0:T(2,128)(2,1)S(1)}, u32[]{:S(2)}, u32[]{:S(2)}) collective-permute-start(bf16[3,2,1024]{2,1,0:T(2,128)(2,1)S(1)} %slice.79), channel_id=1, source_target_pairs={{0,4},{4,8},{8,12},{12,16},{16,20},{20,24},{24,28},{1,5},{5,9},{9,... | collective-permute-start | bytes 36872 | tf_op jit(solution)/shard_map/ppermute | solution.py:11
  14.4 2.3 copy.33
  20.7 2.0 maximum_convert_fusion
  22.7 3.2 %multiply_add_fusion = f32[3,128,1024]{1,2,0:T(8,128)S(1)} fusion(f32[3,130,1024]{1,2,0:T(8,128)S(1)} %maximum_convert_fusion, f32[3,1024]{1,0:T(4,128)S(1)} %get-tuple-element.26, f32[3,1024]{1,0:T(4,128)} %get-tuple-element.27, f32[3,1024]{1,0:T(4,128)S(1)} %bitcast.110), kind=kLoop, calls=%fused_computation.57 | loop fusion | flops 1966080 | bytes 6328320 | tf_op jit(solution)/shard_map/add | solution.py:93
  27.2 2.4 copy.35
  29.6 4.9 %all-to-all-start = ((f32[128,3,1024]{0,1,2:T(4,128)}), f32[128,3,1024]{0,1,2:T(4,128)}, u32[]{:S(2)}, u32[]{:S(2)}) async-start(f32[128,3,1024]{0,1,2:T(4,128)} %copy.35), calls=%async_computation | async-start | bytes 4194304 | tf_op jit(solution)/shard_map/all_to_all | solution.py:32
  34.8 47.8 %all-to-all-done = f32[128,3,1024]{0,1,2:T(4,128)} async-done(((f32[128,3,1024]{0,1,2:T(4,128)}), f32[128,3,1024]{0,1,2:T(4,128)}, u32[]{:S(2)}, u32[]{:S(2)}) %all-to-all-start) | async-done | bytes 1572896 | tf_op jit(solution)/shard_map/all_to_all | solution.py:32
  82.6 5.1 %fusion.41 = f32[3,128,128,16]{2,3,1,0:T(8,128)S(1)} fusion(f32[128,3,8,128]{0,1,3,2:T(4,128)} %bitcast.4), kind=kOutput, calls=%fused_computation.45 | convolution fusion | flops 75499264 | bytes 4718592 | tf_op jit(solution)/shard_map/qm,ncmj->ncqj/dot_general | solution.py:21
  87.7 5.7 %fusion = (f32[3,128,16,128]{3,2,1,0:T(8,128)S(1)}, f32[3,128,16,128]{3,2,1,0:T(8,128)S(1)}) fusion(f32[3,128,128,16]{2,3,1,0:T(8,128)S(1)} %fusion.41, f32[16,128]{1,0:T(8,128)S(1)} %get-tuple-element.28, f32[16,128]{1,0:T(8,128)S(1)} %get-tuple-element.29, f32[128,3,8,128]{0,1,3,2:T(4,128)} %bitcast.4), kind=kOutput, calls=%fused_computation.5 | convolution fusion | flops 81004288 | bytes 11026432 | tf_op jit(solution)/shard_map/qm,ncmj->ncqj/dot_general | solution.py:21
  93.4 3.6 %fusion.18 = f32[3,128,16,128]{3,1,2,0:T(8,128)S(1)} fusion(f32[3,128,16,128]{3,2,1,0:T(8,128)S(1)} %get-tuple-element.13), kind=kOutput, calls=%fused_computation.25 | convolution fusion | flops 1208188928 | bytes 6291456 | tf_op jit(solution)/shard_map/rj,ncqj->ncqr/dot_general | solution.py:21
  97.0 3.9 %fusion.20 = f32[3,128,16,128]{3,1,2,0:T(8,128)S(1)} fusion(f32[3,128,16,128]{3,2,1,0:T(8,128)S(1)} %get-tuple-element.13), kind=kOutput, calls=%fused_computation.27 | convolution fusion | flops 1208188928 | bytes 6291456 | tf_op jit(solution)/shard_map/rj,ncqj->ncqr/dot_general | solution.py:21
  101.0 3.7 %fusion.29 = f32[3,128,16,128]{3,1,2,0:T(8,128)S(1)} fusion(f32[3,128,16,128]{3,1,2,0:T(8,128)S(1)} %fusion.18, f32[3,128,16,128]{3,2,1,0:T(8,128)S(1)} %get-tuple-element.12), kind=kOutput, calls=%fused_computation.34 | convolution fusion | flops 1208975360 | bytes 9437184 | tf_op jit(solution)/shard_map/rj,ncqj->ncqr/dot_general | solution.py:21
  104.6 3.7 %fusion.26 = f32[3,128,16,128]{3,1,2,0:T(8,128)S(1)} fusion(f32[3,128,16,128]{3,1,2,0:T(8,128)S(1)} %fusion.20, f32[3,128,16,128]{3,2,1,0:T(8,128)S(1)} %get-tuple-element.12), kind=kOutput, calls=%fused_computation.33 | convolution fusion | flops 1208975360 | bytes 9437184 | tf_op jit(solution)/shard_map/rj,ncqj->ncqr/dot_general | solution.py:21
  110.7 4.6 %fusion.10 = f32[3,128,16,128]{3,2,1,0:T(8,128)S(1)} fusion(f32[3,128,16,128]{3,1,2,0:T(8,128)S(1)} %pad_maximum_fusion.1), kind=kOutput, calls=%fused_computation.17 | convolution fusion | flops 1208188928 | bytes 6291456 | tf_op jit(solution)/shard_map/rj,ncqr->ncqj/dot_general | solution.py:21
  115.4 4.7 %fusion.12 = f32[3,128,16,128]{3,2,1,0:T(8,128)S(1)} fusion(f32[3,128,16,128]{3,1,2,0:T(8,128)S(1)} %pad_maximum_fusion.1), kind=kOutput, calls=%fused_computation.19 | convolution fusion | flops 1208188928 | bytes 6291456 | tf_op jit(solution)/shard_map/rj,ncqr->ncqj/dot_general | solution.py:21
  120.3 4.8 %fusion.35 = f32[3,128,16,128]{3,2,1,0:T(8,128)S(1)} fusion(f32[3,128,16,128]{3,2,1,0:T(8,128)S(1)} %fusion.10, f32[3,128,16,128]{3,1,2,0:T(8,128)S(1)} %pad_maximum_fusion), kind=kOutput, calls=%fused_computation.36 | convolution fusion | flops 1208975360 | bytes 9437184 | tf_op jit(solution)/shard_map/rj,ncqr->ncqj/dot_general | solution.py:21
  125.1 4.6 %fusion.32 = f32[3,128,16,128]{3,2,1,0:T(8,128)S(1)} fusion(f32[3,128,16,128]{3,2,1,0:T(8,128)S(1)} %fusion.12, f32[3,128,16,128]{3,1,2,0:T(8,128)S(1)} %pad_maximum_fusion), kind=kOutput, calls=%fused_computation.35 | convolution fusion | flops 1208975360 | bytes 9437184 | tf_op jit(solution)/shard_map/rj,ncqr->ncqj/dot_general | solution.py:21
  129.7 2.1 fusion.2
  131.8 2.2 multiply_bitcast_fusion
  134.4 40.7 %all_to_all.17 = f32[8,128,3,128]{1,3,2,0:T(8,128)S(1)} all-to-all(f32[8,128,3,128]{1,3,2,0:T(8,128)S(1)} %copy.46), channel_id=1, replica_groups=mesh['seq'=8,'chan'=4] {'seq'}, dimensions={0} | all-to-all | bytes 3145728 | tf_op jit(solution)/shard_map/all_to_all | solution.py:71
  186.8 2.2 pad_maximum_fusion.2
  189.1 5.2 %multiply_reduce_fusion.2 = (f32[3,1024]{1,0:T(4,128)S(1)}, f32[3,1024]{1,0:T(4,128)S(1)}, f32[3,1024]{1,0:T(4,128)S(1)}, bf16[3,128,1024]{1,2,0:T(8,128)(2,1)}) fusion(f32[3,130,1024]{1,2,0:T(8,128)S(1)} %maximum_convert_fusion, f32[1,128,1024]{1,2,0:T(8,128)S(1)} %copy-done.5, f32[1,128,1024]{1,2,0:T(8,128)S(1)} %copy-done.3, ...), kind=kLoop, calls=%fused_computation.51 | loop fusion | flops 5495808 | bytes 10297344 | tf_op jit(solution)/shard_map/reduce_sum | solution.py:128
  194.3 35.9 %psum.7 = f32[3,3,1024]{2,0,1:T(4,128)S(1)} all-reduce(f32[3,3,1024]{2,0,1:T(4,128)S(1)} %pad_maximum_fusion.5), channel_id=1, replica_groups=mesh['seq'=8,'chan'=4] {'seq'}, use_global_device_ids=true, to_apply=%region_5.6 | all-reduce | flops 9216 | bytes 73728 | tf_op jit(solution)/shard_map/psum | solution.py:130
  230.9 2.3 copy.50
  (58 shorter events, 23.2 us)
Async XLA Ops:
  8.0 11.5 %collective-permute-start = (bf16[3,2,1024]{2,1,0:T(2,128)(2,1)S(1)}, bf16[3,2,1024]{2,1,0:T(2,128)(2,1)S(1)}, u32[]{:S(2)}, u32[]{:S(2)}) collective-permute-start(bf16[3,2,1024]{2,1,0:T(2,128)(2,1)S(1)} %slice.79), channel_id=1, source_target_pairs={{0,4},{4,8},{8,12},{12,16},{16,20},{20,24},{24,28},{1,5},{5,9},{9,... | collective-permute-start | bytes 36872 | tf_op jit(solution)/shard_map/ppermute | solution.py:11
  20.7 2.0 copy-start.10
  25.8 1.2 copy-start
  29.6 52.9 %all-to-all-start = ((f32[128,3,1024]{0,1,2:T(4,128)}), f32[128,3,1024]{0,1,2:T(4,128)}, u32[]{:S(2)}, u32[]{:S(2)}) async-start(f32[128,3,1024]{0,1,2:T(4,128)} %copy.35), calls=%async_computation | async-start | bytes 4194304 | tf_op jit(solution)/shard_map/all_to_all | solution.py:32
  34.5 198.6 %reduce-scatter.2.cloned.1.call-start = ((), (), s32[]{:S(2)}) async-start(), calls=%async_computation.3 | async-start | bytes 163840 | tf_op jit(solution)/shard_map/reduce_scatter | solution.py:116
  134.4 40.9 %copy-start.1 = (f32[3,128,1024]{1,2,0:T(8,128)S(1)}, f32[3,128,1024]{1,2,0:T(8,128)}, u32[]{:S(2)}) copy-start(f32[3,128,1024]{1,2,0:T(8,128)} %copy-done) | copy-start | bytes 4718596
  175.3 2.3 copy-start.8
  175.4 0.9 copy-start.2
  175.4 2.1 copy-start.4
  175.4 2.1 copy-start.6
  179.4 5.7 %collective-permute-start.1 = (f32[3,2,1024]{2,1,0:T(2,128)S(1)}, f32[3,2,1024]{2,1,0:T(2,128)S(1)}, u32[]{:S(2)}, u32[]{:S(2)}) collective-permute-start(f32[3,2,1024]{2,1,0:T(2,128)S(1)} %copy.48), channel_id=1, source_target_pairs={{4,0},{8,4},{12,8},{16,12},{20,16},{24,20},{28,24},{5,1},{9,5},{13... | collective-permute-start | bytes 73736 | tf_op jit(solution)/shard_map/ppermute | solution.py:11
  186.8 2.2 copy-start.3
  186.8 2.2 copy-start.5
  186.8 2.3 copy-start.7
  186.8 2.3 copy-start.9
  186.8 2.3 copy-start.11
Sparse Core Ops, SparseCore 0:
  184.4 19.8 reduce-scatter.1
